TPU v7x, 256 devices: a whole 4x4x8 slice. The times are simulated.
256 devices in a mesh: group: 32 (over z, x), member: 4 (over y), pair: 2 (over core).
Axes of the slice: x: 4, y: 4, z: 8, core: 2. Of those that a mesh axis runs over, the one named last changes fastest.
Arguments:
- tokens: bfloat16 [32768, 768], P(('group', 'member', 'pair')), may hold values from -6 to 6
- out_grad: bfloat16 [32768, 768], P(('group', 'member', 'pair')), may hold values from -6 to 6
- router_gate: float32 [32768], P(('group', 'member', 'pair')), may hold values from 0.2 to 1
- expand_weight: bfloat16 [128, 768, 3072], P(('group', 'member'), None, 'pair'), may hold values from -0.21875 to 0.21875
- shrink_weight: bfloat16 [128, 3072, 768], P(('group', 'member'), 'pair'), may hold values from -0.109375 to 0.109375
- expert_ids: int32 [32768], P(('group', 'member', 'pair')), may hold values from 0 to 127, as said below
- slot_ids: int32 [32768], P(('group', 'member', 'pair')), may hold values from 0 to 1, as said below
- capacity: int32 [128], replicated, may hold values from 1 to 2, as said below
Outputs:
- token_grad: bfloat16 [32768, 768], P(('group', 'member', 'pair'))
- expand_grad: bfloat16 [128, 768, 3072], P(('group', 'member'), None, 'pair')
- shrink_grad: bfloat16 [128, 3072, 768], P(('group', 'member'), 'pair')
Inputs may be any that keep to these rules, and one draw needn't show every extreme that they name: `expert_ids`: in each aligned block of 128 tokens (the tokens of one device) no expert is named by more than 2 tokens, and one expert, the same for all blocks, is named by exactly 2 tokens in every block. `slot_ids`: A token's slot is the number of earlier tokens of its aligned block of 128 that name the same expert. The expert that is named 2 times in every block has capacity 2.
All inputs are finite; a program needn't handle non-finite values.
Results may differ from a plain program's by a relative error of at most 0.0058.
Values may be sent and summed in bfloat16 or wider, within the bound.
A program may use at most 64 MiB of HBM per device.

v0:
```python
import jax
import jax.numpy as jnp
from jax import lax
from jax.sharding import PartitionSpec as P


def activation(value):
    return jax.nn.gelu(value, approximate=True)


def expert_pass(token_rows, grad_rows, expand, shrink):
    f32 = jnp.float32
    preact = jnp.einsum("rd,df->rf", token_rows, expand, preferred_element_type=f32)
    hidden, pullback = jax.vjp(activation, preact)
    hidden_low = hidden.astype(jnp.bfloat16)
    post_grad = jnp.einsum("rd,fd->rf", grad_rows, shrink, preferred_element_type=f32)
    pre_grad = pullback(post_grad)[0].astype(jnp.bfloat16)
    partial_value = jnp.einsum("rf,df->rd", pre_grad, expand, preferred_element_type=f32)
    expand_part = jnp.einsum("rd,rf->df", token_rows, pre_grad, preferred_element_type=f32)
    shrink_part = jnp.einsum("rf,rd->fd", hidden_low, grad_rows, preferred_element_type=f32)
    return (expand_part.astype(jnp.bfloat16), shrink_part.astype(jnp.bfloat16), partial_value)


def per_device(
    tokens, out_grad, router_gate, expand_weight, shrink_weight, expert_ids, slot_ids, capacity
):
    tok_dev, width = tokens.shape
    experts = capacity.shape[0]
    slots = max(2, 2 * tok_dev // experts)
    f32, bf16 = (jnp.float32, jnp.bfloat16)
    table = jnp.arange(experts, dtype=jnp.int32)
    limits = jnp.sum(jnp.where(expert_ids[:, None] == table[None, :], capacity[None, :], 0), axis=1)
    keep = slot_ids < limits
    target = jnp.where(keep, expert_ids * slots + slot_ids, experts * slots)
    place = (jnp.arange(experts * slots, dtype=jnp.int32)[:, None] == target[None, :]).astype(bf16)
    scaled = (router_gate[:, None] * out_grad.astype(f32)).astype(bf16)
    token_send = jnp.dot(place, tokens, preferred_element_type=f32).astype(bf16)
    grad_send = jnp.dot(place, scaled, preferred_element_type=f32).astype(bf16)
    token_send = token_send.reshape(experts, slots, width)
    grad_send = grad_send.reshape(experts, slots, width)
    axes = ("group", "member")
    token_rows = lax.all_to_all(token_send, axes, split_axis=0, concat_axis=0, tiled=True)
    grad_rows = lax.all_to_all(grad_send, axes, split_axis=0, concat_axis=0, tiled=True)
    token_rows = lax.all_gather(token_rows.reshape(-1, width), "pair", axis=0, tiled=True)
    grad_rows = lax.all_gather(grad_rows.reshape(-1, width), "pair", axis=0, tiled=True)
    expand_grad, shrink_grad, partial_value = expert_pass(
        token_rows, grad_rows, expand_weight[0], shrink_weight[0]
    )
    rows = experts * slots
    me = lax.axis_index("pair")
    halves = partial_value.reshape(2, rows, width)
    other = lax.ppermute(
        lax.dynamic_index_in_dim(halves, 1 - me, 0, keepdims=False), "pair", ((0, 1), (1, 0))
    )
    summed = lax.dynamic_index_in_dim(halves, me, 0, keepdims=False) + other
    back = summed.astype(bf16).reshape(experts, slots, width)
    back = lax.all_to_all(back, axes, split_axis=0, concat_axis=0, tiled=True)
    token_grad = lax.dot_general(
        place, back.reshape(rows, width), (((0,), (0,)), ((), ())), preferred_element_type=f32
    ).astype(bf16)
    return (token_grad, expand_grad[None], shrink_grad[None])


def solution(mesh):
    placed = (
        P(("group", "member", "pair"), None),
        P(("group", "member", "pair"), None),
        P(("group", "member", "pair")),
        P(("group", "member"), None, "pair"),
        P(("group", "member"), "pair", None),
        P(("group", "member", "pair")),
        P(("group", "member", "pair")),
        P(),
    )
    return jax.shard_map(
        per_device,
        mesh=mesh,
        in_specs=placed,
        out_specs=(
            P(("group", "member", "pair"), None),
            P(("group", "member"), None, "pair"),
            P(("group", "member"), "pair", None),
        ),
        check_vma=False,
    )
```

profile of v0, /device:TPU:1, one launch (start us, length us, event | category | flops | bytes accessed | tf_op | source)
XLA Modules:
  0.0 102.9 jit_solution(17785780471842416386)
XLA Ops:
  0.6 1.0 select_reduce_fusion
  2.3 1.2 %convolution_convert_fusion.2 = bf16[256,768]{1,0:T(8,128)(2,1)S(1)} fusion(bf16[128,768]{1,0:T(8,128)(2,1)} %param.8, s32[128]{0:T(128)S(1)} %compare_select_fusion), kind=kOutput, calls=%fused_computation.24 | convolution fusion | flops 50561024 | bytes 590336 | tf_op jit(solution)/shard_map/dot_general | solution.py:37
  3.5 0.9 reshape.32
  4.4 16.3 %all-to-all-start.1 = ((bf16[128,2,768]{2,1,0:T(2,128)(2,1)}), bf16[128,2,768]{2,1,0:T(2,128)(2,1)S(1)}, u32[]{:S(2)}, u32[]{:S(2)}) async-start(bf16[128,2,768]{2,1,0:T(2,128)(2,1)} %reshape.32), calls=%async_computation.1 | async-start | bytes 786432 | tf_op jit(solution)/shard_map/all_to_all | solution.py:42
  20.7 1.3 %convolution_convert_fusion.3 = bf16[256,768]{1,0:T(8,128)(2,1)S(1)} fusion(bf16[128,768]{1,0:T(8,128)(2,1)} %param.9, f32[128]{0:T(128)} %param.10, s32[128]{0:T(128)S(1)} %compare_select_fusion), kind=kOutput, calls=%fused_computation.25 | convolution fusion | flops 50855936 | bytes 590848 | tf_op jit(solution)/shard_map/dot_general | solution.py:38
  22.0 0.9 reshape.30
  22.9 13.8 %all-to-all-done.1 = bf16[128,2,768]{2,1,0:T(2,128)(2,1)S(1)} async-done(((bf16[128,2,768]{2,1,0:T(2,128)(2,1)}), bf16[128,2,768]{2,1,0:T(2,128)(2,1)S(1)}, u32[]{:S(2)}, u32[]{:S(2)}) %all-to-all-start.1) | async-done | bytes 393248 | tf_op jit(solution)/shard_map/all_to_all | solution.py:42
  36.7 6.8 %all-to-all-start = ((bf16[128,2,768]{2,1,0:T(2,128)(2,1)}), bf16[128,2,768]{2,1,0:T(2,128)(2,1)S(1)}, u32[]{:S(2)}, u32[]{:S(2)}) async-start(bf16[128,2,768]{2,1,0:T(2,128)(2,1)} %reshape.30), calls=%async_computation | async-start | bytes 786432 | tf_op jit(solution)/shard_map/all_to_all | solution.py:43
  43.7 4.4 %all_gather.7 = bf16[512,768]{1,0:T(8,128)(2,1)} all-gather(bf16[256,768]{1,0:T(8,128)(2,1)S(1)} %reshape.33), channel_id=1, replica_groups=mesh['group'=32,'member'=4,'pair'=2] {'pair'}, dimensions={0}, use_global_device_ids=true | all-gather | bytes 1179648 | tf_op jit(solution)/shard_map/all_gather | solution.py:44
  48.1 9.8 %all-to-all-done = bf16[128,2,768]{2,1,0:T(2,128)(2,1)S(1)} async-done(((bf16[128,2,768]{2,1,0:T(2,128)(2,1)}), bf16[128,2,768]{2,1,0:T(2,128)(2,1)S(1)}, u32[]{:S(2)}, u32[]{:S(2)}) %all-to-all-start) | async-done | bytes 393248 | tf_op jit(solution)/shard_map/all_to_all | solution.py:43
  58.1 6.4 %all_gather.6 = bf16[512,768]{1,0:T(8,128)(2,1)S(1)} all-gather(bf16[256,768]{1,0:T(8,128)(2,1)S(1)} %reshape.31), channel_id=1, replica_groups=mesh['group'=32,'member'=4,'pair'=2] {'pair'}, dimensions={0}, use_global_device_ids=true | all-gather | bytes 1179648 | tf_op jit(solution)/shard_map/all_gather | solution.py:45
  64.5 2.9 %fusion.11 = f32[512,1536]{1,0:T(8,128)S(1)} fusion(bf16[512,768]{1,0:T(8,128)(2,1)} %all_gather.7, bf16[1,768,1536]{2,1,0:T(8,128)(2,1)S(1)} %copy-done), kind=kOutput, calls=%fused_computation.16 | convolution fusion | flops 1207959552 | bytes 6291456 | tf_op jit(solution)/shard_map/rd,df->rf/dot_general | solution.py:13
  67.4 3.1 %fusion.6 = bf16[512,1536]{1,0:T(8,128)(2,1)S(1)} fusion(f32[512,1536]{1,0:T(8,128)S(1)} %fusion.11, bf16[512,768]{1,0:T(8,128)(2,1)S(1)} %all_gather.6, bf16[1,1536,768]{2,1,0:T(8,128)(2,1)S(1)} %copy-done.5), kind=kOutput, calls=%fused_computation.10 | convolution fusion | flops 1223688192 | bytes 7864320 | tf_op jit(solution)/shard_map/rd,fd->rf/dot_general | solution.py:16
  70.5 1.4 %fusion.9 = f32[2,256,768]{2,1,0:T(8,128)S(1)} fusion(bf16[2,256,1536]{2,1,0:T(8,128)(2,1)S(1)} %bitcast.30, bf16[1,768,1536]{2,1,0:T(8,128)(2,1)S(1)} %copy-done), kind=kOutput, calls=%fused_computation.14 | convolution fusion | flops 1207959552 | bytes 5505024 | tf_op jit(solution)/shard_map/rf,df->rd/dot_general | solution.py:18
  72.0 1.1 %copy-done.1 = f32[2,256,768]{2,1,0:T(8,128)} copy-done((f32[2,256,768]{2,1,0:T(8,128)}, f32[2,256,768]{2,1,0:T(8,128)S(1)}, u32[]{:S(2)}) %copy-start.1) | copy-done | bytes 1572888
  73.1 0.9 dynamic-slice_bitcast_fusion
  74.4 2.3 %collective-permute-done = f32[256,768]{1,0:T(8,128)} collective-permute-done((f32[256,768]{1,0:T(8,128)}, f32[256,768]{1,0:T(8,128)}, u32[]{:S(2)}, u32[]{:S(2)}) %collective-permute-start) | collective-permute-done | bytes 786464 | tf_op jit(solution)/shard_map/ppermute | solution.py:52
  76.7 1.4 %fusion.21 = bf16[256,768]{1,0:T(8,128)(2,1)S(1)} fusion(f32[256,768]{1,0:T(8,128)} %collective-permute-done, f32[2,256,768]{2,1,0:T(8,128)} %copy-done.1, s32[]{:T(128)S(6)} %select_n.17), kind=kLoop, calls=%fused_computation.28 | loop fusion | flops 393216 | bytes 1966084 | tf_op jit(solution)/shard_map/convert_element_type | solution.py:56
  78.1 0.9 reshape.34
  79.0 6.3 %all-to-all-start.2 = ((bf16[128,2,768]{2,1,0:T(2,128)(2,1)}), bf16[128,2,768]{2,1,0:T(2,128)(2,1)S(1)}, u32[]{:S(2)}, u32[]{:S(2)}) async-start(bf16[128,2,768]{2,1,0:T(2,128)(2,1)} %reshape.34), calls=%async_computation.2 | async-start | bytes 786432 | tf_op jit(solution)/shard_map/all_to_all | solution.py:57
  85.4 4.4 %fusion.7 = bf16[1,768,1536]{2,1,0:T(8,128)(2,1)} fusion(bf16[512,768]{1,0:T(8,128)(2,1)S(1)} %copy-done.2, bf16[512,1536]{1,0:T(8,128)(2,1)} %copy-done.6), kind=kOutput, calls=%fused_computation.12 | convolution fusion | flops 1209139200 | bytes 4718592 | tf_op jit(solution)/shard_map/rd,rf->df/dot_general | solution.py:19
  89.8 3.2 %fusion.8 = bf16[1,1536,768]{2,1,0:T(8,128)(2,1)} fusion(bf16[512,768]{1,0:T(8,128)(2,1)S(1)} %copy-done.4, f32[512,1536]{1,0:T(8,128)S(1)} %copy-done.8), kind=kOutput, calls=%fused_computation.13 | convolution fusion | flops 1216217088 | bytes 6291456 | tf_op jit(solution)/shard_map/rf,rd->fd/dot_general | solution.py:20
  93.0 8.8 %all-to-all-done.2 = bf16[128,2,768]{2,1,0:T(2,128)(2,1)S(1)} async-done(((bf16[128,2,768]{2,1,0:T(2,128)(2,1)}), bf16[128,2,768]{2,1,0:T(2,128)(2,1)S(1)}, u32[]{:S(2)}, u32[]{:S(2)}) %all-to-all-start.2) | async-done | bytes 393248 | tf_op jit(solution)/shard_map/all_to_all | solution.py:57
  101.9 0.9 convolution_convert_fusion.4
  (22 shorter events, 1.5 us)
Async XLA Ops:
  0.6 63.9 %copy-start = (bf16[1,768,1536]{2,1,0:T(8,128)(2,1)S(1)}, bf16[1,768,1536]{2,1,0:T(8,128)(2,1)}, u32[]{:S(2)}) copy-start(bf16[1,768,1536]{2,1,0:T(8,128)(2,1)} %param.11) | copy-start | bytes 7077892
  4.4 32.3 %all-to-all-start.1 = ((bf16[128,2,768]{2,1,0:T(2,128)(2,1)}), bf16[128,2,768]{2,1,0:T(2,128)(2,1)S(1)}, u32[]{:S(2)}, u32[]{:S(2)}) async-start(bf16[128,2,768]{2,1,0:T(2,128)(2,1)} %reshape.32), calls=%async_computation.1 | async-start | bytes 786432 | tf_op jit(solution)/shard_map/all_to_all | solution.py:42
  36.7 21.3 %all-to-all-start = ((bf16[128,2,768]{2,1,0:T(2,128)(2,1)}), bf16[128,2,768]{2,1,0:T(2,128)(2,1)S(1)}, u32[]{:S(2)}, u32[]{:S(2)}) async-start(bf16[128,2,768]{2,1,0:T(2,128)(2,1)} %reshape.30), calls=%async_computation | async-start | bytes 786432 | tf_op jit(solution)/shard_map/all_to_all | solution.py:43
  64.5 2.9 %copy-start.3 = (bf16[512,768]{1,0:T(8,128)(2,1)}, bf16[512,768]{1,0:T(8,128)(2,1)S(1)}, u32[]{:S(2)}) copy-start(bf16[512,768]{1,0:T(8,128)(2,1)S(1)} %all_gather.6) | copy-start | bytes 2359300
  64.5 2.9 %copy-start.5 = (bf16[1,1536,768]{2,1,0:T(8,128)(2,1)S(1)}, bf16[1,1536,768]{2,1,0:T(8,128)(2,1)}, u32[]{:S(2)}) copy-start(bf16[1,1536,768]{2,1,0:T(8,128)(2,1)} %param.12) | copy-start | bytes 7077892
  67.4 3.1 %copy-start.7 = (f32[512,1536]{1,0:T(8,128)}, f32[512,1536]{1,0:T(8,128)S(1)}, u32[]{:S(2)}) copy-start(f32[512,1536]{1,0:T(8,128)S(1)} %fusion.11) | copy-start | bytes 9437188
  70.5 1.4 %copy-start.6 = (bf16[512,1536]{1,0:T(8,128)(2,1)}, bf16[512,1536]{1,0:T(8,128)(2,1)S(1)}, u32[]{:S(2)}) copy-start(bf16[512,1536]{1,0:T(8,128)(2,1)S(1)} %fusion.6) | copy-start | bytes 4718596
  72.0 1.1 %copy-start.1 = (f32[2,256,768]{2,1,0:T(8,128)}, f32[2,256,768]{2,1,0:T(8,128)S(1)}, u32[]{:S(2)}) copy-start(f32[2,256,768]{2,1,0:T(8,128)S(1)} %fusion.9) | copy-start | bytes 4718596
  73.1 12.3 %copy-start.2 = (bf16[512,768]{1,0:T(8,128)(2,1)S(1)}, bf16[512,768]{1,0:T(8,128)(2,1)}, u32[]{:S(2)}) copy-start(bf16[512,768]{1,0:T(8,128)(2,1)} %all_gather.7) | copy-start | bytes 2359300
  74.0 2.6 %collective-permute-start = (f32[256,768]{1,0:T(8,128)}, f32[256,768]{1,0:T(8,128)}, u32[]{:S(2)}, u32[]{:S(2)}) collective-permute-start(f32[256,768]{1,0:T(8,128)} %dynamic-slice_bitcast_fusion), channel_id=1, source_target_pairs={{0,1},{1,0},{2,3},{3,2},{4,5},{5,4},{6,7},{7,6},{8,9},{9,8},{10,11... | collective-permute-start | bytes 2359304 | tf_op jit(solution)/shard_map/ppermute | solution.py:52
  79.0 22.8 %all-to-all-start.2 = ((bf16[128,2,768]{2,1,0:T(2,128)(2,1)}), bf16[128,2,768]{2,1,0:T(2,128)(2,1)S(1)}, u32[]{:S(2)}, u32[]{:S(2)}) async-start(bf16[128,2,768]{2,1,0:T(2,128)(2,1)} %reshape.34), calls=%async_computation.2 | async-start | bytes 786432 | tf_op jit(solution)/shard_map/all_to_all | solution.py:57
  85.4 4.4 %copy-start.4 = (bf16[512,768]{1,0:T(8,128)(2,1)S(1)}, bf16[512,768]{1,0:T(8,128)(2,1)}, u32[]{:S(2)}) copy-start(bf16[512,768]{1,0:T(8,128)(2,1)} %copy-done.3) | copy-start | bytes 2359300
  85.4 4.4 %copy-start.8 = (f32[512,1536]{1,0:T(8,128)S(1)}, f32[512,1536]{1,0:T(8,128)}, u32[]{:S(2)}) copy-start(f32[512,1536]{1,0:T(8,128)} %copy-done.7) | copy-start | bytes 9437188
where the time goes:
time: 103 us
  waiting for transfers between devices  34.7 us (34%)
  starting transfers between devices  29.9 us (29%)
  matrix products  18.2 us (18%)
  blocking collectives  10.9 us (11%)
  local copies, waits for them, and re-layouts  5.25 us (5%)
  other arithmetic  3.12 us (3%)
    all_to_all x1, starting transfers between devices, per_device(): lax.all_to_all(token_send, axes, split_axis=0, concat_axis=0, tiled=True)  16.3 us
    all_to_all x1, waiting for transfers between devices, per_device(): lax.all_to_all(token_send, axes, split_axis=0, concat_axis=0, tiled=True)  13.8 us
    all_to_all x1, waiting for transfers between devices, per_device(): lax.all_to_all(grad_send, axes, split_axis=0, concat_axis=0, tiled=True)  9.84 us
    all_to_all x1, waiting for transfers between devices, per_device(): back = lax.all_to_all(back, axes, split_axis=0, concat_axis=0, tiled=True)  8.84 us
    all_to_all x1, starting transfers between devices, per_device(): lax.all_to_all(grad_send, axes, split_axis=0, concat_axis=0, tiled=True)  6.83 us
    all_gather x1, blocking collectives, per_device(): lax.all_gather(grad_rows.reshape(-1, width), 'pair', axis=0, tiled=True)  6.43 us
    all_to_all x1, starting transfers between devices, per_device(): back = lax.all_to_all(back, axes, split_axis=0, concat_axis=0, tiled=True)  6.35 us
    all_gather x1, blocking collectives, per_device(): lax.all_gather(token_rows.reshape(-1, width), 'pair', axis=0, tiled=True)  4.44 us
  transfers between devices with their start and end apart: 4, of which 4 were waited for; matrix products, arithmetic and copies ran while one was open for 10% of the time, Pallas kernels for 0%

commit v1 on v0

--- a/solution.py
+++ b/solution.py
@@ -42,7 +42,12 @@
     token_rows = lax.all_to_all(token_send, axes, split_axis=0, concat_axis=0, tiled=True)
     grad_rows = lax.all_to_all(grad_send, axes, split_axis=0, concat_axis=0, tiled=True)
     token_rows = lax.all_gather(token_rows.reshape(-1, width), "pair", axis=0, tiled=True)
-    grad_rows = lax.all_gather(grad_rows.reshape(-1, width), "pair", axis=0, tiled=True)
+    grad_rows = jnp.concatenate(
+        lax.all_to_all(
+            jnp.stack([grad_rows.reshape(-1, width)] * lax.axis_size("pair")), "pair", 0, 0
+        ),
+        axis=0,
+    )
     expand_grad, shrink_grad, partial_value = expert_pass(
         token_rows, grad_rows, expand_weight[0], shrink_weight[0]
     )

time: 103 us -> 110 us (1.068)
  starting transfers between devices: 29.9 us -> 37.5 us
  blocking collectives: 10.9 us -> 4.44 us
  matrix products: 18.2 us -> 21.8 us
    all_to_all x0 -> x1, starting transfers between devices: none -> 7.96 us  [per_device(): lax.all_to_all(jnp.stack([grad_rows.reshape(-1, width)] * lax.axis_size('...]
    all_gather x1 -> x0, blocking collectives: 6.43 us -> none  [per_device(): lax.all_gather(grad_rows.reshape(-1, width), 'pair', axis=0, tiled=True)]
    dot_general x1, matrix products: 3.07 us -> 5.32 us  [expert_pass(): jnp.einsum('rd,fd->rf', grad_rows, shrink, preferred_element_type=f32)]
    dot_general x1, matrix products: 2.85 us -> 4.15 us  [expert_pass(): jnp.einsum('rd,df->rf', token_rows, expand, preferred_element_type=f32)]
  transfers between devices with their start and end apart: 4 -> 5, of which waited for: 4 -> 4; matrix products, arithmetic and copies ran while one was open for 10% -> 13% of each run, Pallas kernels for 0% -> 0%
where the time goes in v1:
time: 110 us; the launch traced here: 109 us
  starting transfers between devices  37.5 us (34%)
  waiting for transfers between devices  35.3 us (32%)
  matrix products  21.8 us (20%)
  local copies, waits for them, and re-layouts  5.24 us (5%)
  blocking collectives  4.44 us (4%)
  other arithmetic  4.06 us (4%)
    all_to_all x1, starting transfers between devices, per_device(): lax.all_to_all(token_send, axes, split_axis=0, concat_axis=0, tiled=True)  16.3 us
    all_to_all x1, waiting for transfers between devices, per_device(): lax.all_to_all(token_send, axes, split_axis=0, concat_axis=0, tiled=True)  13.8 us
    all_to_all x1, waiting for transfers between devices, per_device(): lax.all_to_all(grad_send, axes, split_axis=0, concat_axis=0, tiled=True)  9.84 us
    all_to_all x1, waiting for transfers between devices, per_device(): back = lax.all_to_all(back, axes, split_axis=0, concat_axis=0, tiled=True)  9.06 us
    all_to_all x1, starting transfers between devices, per_device(): lax.all_to_all(jnp.stack([grad_rows.reshape(-1, width)] * lax.axis_size('...  7.96 us
    all_to_all x1, starting transfers between devices, per_device(): lax.all_to_all(grad_send, axes, split_axis=0, concat_axis=0, tiled=True)  6.83 us
    all_to_all x1, starting transfers between devices, per_device(): back = lax.all_to_all(back, axes, split_axis=0, concat_axis=0, tiled=True)  6.35 us
    dot_general x1, matrix products, expert_pass(): jnp.einsum('rd,fd->rf', grad_rows, shrink, preferred_element_type=f32)  5.32 us
  transfers between devices with their start and end apart: 5, of which 4 were waited for; matrix products, arithmetic and copies ran while one was open for 13% of the time, Pallas kernels for 0%

profile of v1, /device:TPU:1, one launch (start us, length us, event | category | flops | bytes accessed | tf_op | source)
XLA Modules:
  0.0 109.1 jit_solution(6240009053933556374)
XLA Ops:
  0.6 1.0 select_reduce_fusion
  2.3 1.2 %convolution_convert_fusion.2 = bf16[256,768]{1,0:T(8,128)(2,1)S(1)} fusion(bf16[128,768]{1,0:T(8,128)(2,1)} %param.8, s32[128]{0:T(128)S(1)} %compare_select_fusion), kind=kOutput, calls=%fused_computation.24 | convolution fusion | flops 50561024 | bytes 590336 | tf_op jit(solution)/shard_map/dot_general | solution.py:37
  3.5 0.9 reshape.32
  4.4 16.3 %all-to-all-start.2 = ((bf16[128,2,768]{2,1,0:T(2,128)(2,1)}), bf16[128,2,768]{2,1,0:T(2,128)(2,1)S(1)}, u32[]{:S(2)}, u32[]{:S(2)}) async-start(bf16[128,2,768]{2,1,0:T(2,128)(2,1)} %reshape.32), calls=%async_computation.2 | async-start | bytes 786432 | tf_op jit(solution)/shard_map/all_to_all | solution.py:42
  20.7 1.3 %convolution_convert_fusion.3 = bf16[256,768]{1,0:T(8,128)(2,1)S(1)} fusion(bf16[128,768]{1,0:T(8,128)(2,1)} %param.9, f32[128]{0:T(128)} %param.10, s32[128]{0:T(128)S(1)} %compare_select_fusion), kind=kOutput, calls=%fused_computation.25 | convolution fusion | flops 50855936 | bytes 590848 | tf_op jit(solution)/shard_map/dot_general | solution.py:38
  22.9 13.8 %all-to-all-done.2 = bf16[128,2,768]{2,1,0:T(2,128)(2,1)S(1)} async-done(((bf16[128,2,768]{2,1,0:T(2,128)(2,1)}), bf16[128,2,768]{2,1,0:T(2,128)(2,1)S(1)}, u32[]{:S(2)}, u32[]{:S(2)}) %all-to-all-start.2) | async-done | bytes 393248 | tf_op jit(solution)/shard_map/all_to_all | solution.py:42
  36.7 6.8 %all-to-all-start = ((bf16[128,2,768]{2,1,0:T(2,128)(2,1)}), bf16[128,2,768]{2,1,0:T(2,128)(2,1)S(1)}, u32[]{:S(2)}, u32[]{:S(2)}) async-start(bf16[128,2,768]{2,1,0:T(2,128)(2,1)} %reshape.30), calls=%async_computation | async-start | bytes 786432 | tf_op jit(solution)/shard_map/all_to_all | solution.py:43
  43.7 4.4 %all_gather.3 = bf16[512,768]{1,0:T(8,128)(2,1)} all-gather(bf16[256,768]{1,0:T(8,128)(2,1)S(1)} %reshape.33), channel_id=1, replica_groups=mesh['group'=32,'member'=4,'pair'=2] {'pair'}, dimensions={0}, use_global_device_ids=true | all-gather | bytes 1179648 | tf_op jit(solution)/shard_map/all_gather | solution.py:44
  48.1 9.8 %all-to-all-done = bf16[128,2,768]{2,1,0:T(2,128)(2,1)S(1)} async-done(((bf16[128,2,768]{2,1,0:T(2,128)(2,1)}), bf16[128,2,768]{2,1,0:T(2,128)(2,1)S(1)}, u32[]{:S(2)}, u32[]{:S(2)}) %all-to-all-start) | async-done | bytes 393248 | tf_op jit(solution)/shard_map/all_to_all | solution.py:43
  58.1 0.9 pad_maximum_fusion
  59.0 8.0 %all-to-all-start.1 = ((bf16[2,256,768]{2,1,0:T(8,128)(2,1)}), bf16[2,256,768]{2,1,0:T(8,128)(2,1)S(1)}, u32[]{:S(2)}, u32[]{:S(2)}) async-start(bf16[2,256,768]{2,1,0:T(8,128)(2,1)} %pad_maximum_fusion), calls=%async_computation.1 | async-start | bytes 1572864 | tf_op jit(solution)/shard_map/all_to_all | solution.py:46
  67.0 4.2 %fusion.11 = f32[512,1536]{1,0:T(8,128)} fusion(bf16[512,768]{1,0:T(8,128)(2,1)} %all_gather.3, bf16[1,768,1536]{2,1,0:T(8,128)(2,1)S(1)} %copy-done), kind=kOutput, calls=%fused_computation.16 | convolution fusion | flops 1207959552 | bytes 6291456 | tf_op jit(solution)/shard_map/rd,df->rf/dot_general | solution.py:13
  71.2 5.3 %fusion.6 = bf16[512,1536]{1,0:T(8,128)(2,1)S(1)} fusion(f32[512,1536]{1,0:T(8,128)} %fusion.11, bf16[512,768]{1,0:T(8,128)(2,1)S(1)} %bitcast.31, bf16[1,1536,768]{2,1,0:T(8,128)(2,1)} %param.12), kind=kOutput, calls=%fused_computation.10 | convolution fusion | flops 1223688192 | bytes 7864320 | tf_op jit(solution)/shard_map/rd,fd->rf/dot_general | solution.py:16
  76.5 1.4 %fusion.9 = f32[2,256,768]{2,1,0:T(8,128)S(1)} fusion(bf16[2,256,1536]{2,1,0:T(8,128)(2,1)S(1)} %bitcast.33, bf16[1,768,1536]{2,1,0:T(8,128)(2,1)S(1)} %copy-done), kind=kOutput, calls=%fused_computation.14 | convolution fusion | flops 1207959552 | bytes 5505024 | tf_op jit(solution)/shard_map/rf,df->rd/dot_general | solution.py:18
  78.0 1.1 %copy-done.1 = f32[2,256,768]{2,1,0:T(8,128)} copy-done((f32[2,256,768]{2,1,0:T(8,128)}, f32[2,256,768]{2,1,0:T(8,128)S(1)}, u32[]{:S(2)}) %copy-start.1) | copy-done | bytes 1572888
  79.1 0.9 dynamic-slice_bitcast_fusion
  80.1 2.6 %collective-permute-done = f32[256,768]{1,0:T(8,128)} collective-permute-done((f32[256,768]{1,0:T(8,128)}, f32[256,768]{1,0:T(8,128)}, u32[]{:S(2)}, u32[]{:S(2)}) %collective-permute-start) | collective-permute-done | bytes 786464 | tf_op jit(solution)/shard_map/ppermute | solution.py:57
  82.7 1.4 %fusion.21 = bf16[256,768]{1,0:T(8,128)(2,1)S(1)} fusion(f32[256,768]{1,0:T(8,128)} %collective-permute-done, f32[2,256,768]{2,1,0:T(8,128)} %copy-done.1, s32[]{:T(128)S(6)} %select_n.17), kind=kLoop, calls=%fused_computation.29 | loop fusion | flops 393216 | bytes 1966084 | tf_op jit(solution)/shard_map/convert_element_type | solution.py:61
  84.1 0.9 reshape.34
  85.0 6.3 %all-to-all-start.3 = ((bf16[128,2,768]{2,1,0:T(2,128)(2,1)}), bf16[128,2,768]{2,1,0:T(2,128)(2,1)S(1)}, u32[]{:S(2)}, u32[]{:S(2)}) async-start(bf16[128,2,768]{2,1,0:T(2,128)(2,1)} %reshape.34), calls=%async_computation.3 | async-start | bytes 786432 | tf_op jit(solution)/shard_map/all_to_all | solution.py:62
  91.4 4.4 %fusion.7 = bf16[1,768,1536]{2,1,0:T(8,128)(2,1)} fusion(bf16[512,768]{1,0:T(8,128)(2,1)S(1)} %copy-done.2, bf16[512,1536]{1,0:T(8,128)(2,1)} %copy-done.5), kind=kOutput, calls=%fused_computation.12 | convolution fusion | flops 1209139200 | bytes 4718592 | tf_op jit(solution)/shard_map/rd,rf->df/dot_general | solution.py:19
  95.8 3.2 %fusion.8 = bf16[1,1536,768]{2,1,0:T(8,128)(2,1)} fusion(bf16[512,768]{1,0:T(8,128)(2,1)S(1)} %bitcast.32, f32[512,1536]{1,0:T(8,128)S(1)} %copy-done.6), kind=kOutput, calls=%fused_computation.13 | convolution fusion | flops 1216217088 | bytes 6291456 | tf_op jit(solution)/shard_map/rf,rd->fd/dot_general | solution.py:20
  98.9 9.1 %all-to-all-done.3 = bf16[128,2,768]{2,1,0:T(2,128)(2,1)S(1)} async-done(((bf16[128,2,768]{2,1,0:T(2,128)(2,1)}), bf16[128,2,768]{2,1,0:T(2,128)(2,1)S(1)}, u32[]{:S(2)}, u32[]{:S(2)}) %all-to-all-start.3) | async-done | bytes 393248 | tf_op jit(solution)/shard_map/all_to_all | solution.py:62
  108.1 0.9 convolution_convert_fusion.4
  (20 shorter events, 2.1 us)
Async XLA Ops:
  0.6 66.4 %copy-start = (bf16[1,768,1536]{2,1,0:T(8,128)(2,1)S(1)}, bf16[1,768,1536]{2,1,0:T(8,128)(2,1)}, u32[]{:S(2)}) copy-start(bf16[1,768,1536]{2,1,0:T(8,128)(2,1)} %param.11) | copy-start | bytes 7077892
  4.4 32.3 %all-to-all-start.2 = ((bf16[128,2,768]{2,1,0:T(2,128)(2,1)}), bf16[128,2,768]{2,1,0:T(2,128)(2,1)S(1)}, u32[]{:S(2)}, u32[]{:S(2)}) async-start(bf16[128,2,768]{2,1,0:T(2,128)(2,1)} %reshape.32), calls=%async_computation.2 | async-start | bytes 786432 | tf_op jit(solution)/shard_map/all_to_all | solution.py:42
  36.7 21.3 %all-to-all-start = ((bf16[128,2,768]{2,1,0:T(2,128)(2,1)}), bf16[128,2,768]{2,1,0:T(2,128)(2,1)S(1)}, u32[]{:S(2)}, u32[]{:S(2)}) async-start(bf16[128,2,768]{2,1,0:T(2,128)(2,1)} %reshape.30), calls=%async_computation | async-start | bytes 786432 | tf_op jit(solution)/shard_map/all_to_all | solution.py:43
  59.0 12.1 %all-to-all-start.1 = ((bf16[2,256,768]{2,1,0:T(8,128)(2,1)}), bf16[2,256,768]{2,1,0:T(8,128)(2,1)S(1)}, u32[]{:S(2)}, u32[]{:S(2)}) async-start(bf16[2,256,768]{2,1,0:T(8,128)(2,1)} %pad_maximum_fusion), calls=%async_computation.1 | async-start | bytes 1572864 | tf_op jit(solution)/shard_map/all_to_all | solution.py:46
  71.2 5.3 %copy-start.3 = (bf16[2,256,768]{2,1,0:T(8,128)(2,1)}, bf16[2,256,768]{2,1,0:T(8,128)(2,1)S(1)}, u32[]{:S(2)}) copy-start(bf16[2,256,768]{2,1,0:T(8,128)(2,1)S(1)} %all-to-all-done.1) | copy-start | bytes 2359300
  76.5 1.4 %copy-start.5 = (bf16[512,1536]{1,0:T(8,128)(2,1)}, bf16[512,1536]{1,0:T(8,128)(2,1)S(1)}, u32[]{:S(2)}) copy-start(bf16[512,1536]{1,0:T(8,128)(2,1)S(1)} %fusion.6) | copy-start | bytes 4718596
  77.9 1.1 %copy-start.1 = (f32[2,256,768]{2,1,0:T(8,128)}, f32[2,256,768]{2,1,0:T(8,128)S(1)}, u32[]{:S(2)}) copy-start(f32[2,256,768]{2,1,0:T(8,128)S(1)} %fusion.9) | copy-start | bytes 4718596
  79.1 12.3 %copy-start.2 = (bf16[512,768]{1,0:T(8,128)(2,1)S(1)}, bf16[512,768]{1,0:T(8,128)(2,1)}, u32[]{:S(2)}) copy-start(bf16[512,768]{1,0:T(8,128)(2,1)} %all_gather.3) | copy-start | bytes 2359300
  80.0 2.6 %collective-permute-start = (f32[256,768]{1,0:T(8,128)}, f32[256,768]{1,0:T(8,128)}, u32[]{:S(2)}, u32[]{:S(2)}) collective-permute-start(f32[256,768]{1,0:T(8,128)} %dynamic-slice_bitcast_fusion), channel_id=1, source_target_pairs={{0,1},{1,0},{2,3},{3,2},{4,5},{5,4},{6,7},{7,6},{8,9},{9,8},{10,11... | collective-permute-start | bytes 2359304 | tf_op jit(solution)/shard_map/ppermute | solution.py:57
  85.0 23.0 %all-to-all-start.3 = ((bf16[128,2,768]{2,1,0:T(2,128)(2,1)}), bf16[128,2,768]{2,1,0:T(2,128)(2,1)S(1)}, u32[]{:S(2)}, u32[]{:S(2)}) async-start(bf16[128,2,768]{2,1,0:T(2,128)(2,1)} %reshape.34), calls=%async_computation.3 | async-start | bytes 786432 | tf_op jit(solution)/shard_map/all_to_all | solution.py:62
  91.4 4.4 %copy-start.4 = (bf16[2,256,768]{2,1,0:T(8,128)(2,1)S(1)}, bf16[2,256,768]{2,1,0:T(8,128)(2,1)}, u32[]{:S(2)}) copy-start(bf16[2,256,768]{2,1,0:T(8,128)(2,1)} %copy-done.3) | copy-start | bytes 2359300
  91.4 4.4 %copy-start.6 = (f32[512,1536]{1,0:T(8,128)S(1)}, f32[512,1536]{1,0:T(8,128)}, u32[]{:S(2)}) copy-start(f32[512,1536]{1,0:T(8,128)} %fusion.11) | copy-start | bytes 9437188
